TPU v7x, 32 devices: a whole 2x2x4 slice. The times are simulated.
32 devices in a mesh: seq: 8 (over y, x, core), grp: 4 (over z).
Axes of the slice: x: 2, y: 2, z: 4, core: 2. Of those that a mesh axis runs over, the one named last changes fastest.
Arguments:
- queries: bfloat16 [8192, 4096], P(('grp', 'seq')), parts along dimension 0, may hold values from -64 to 64
- keys: bfloat16 [8192, 1024], P(('grp', 'seq')), parts along dimension 0, may hold values from -64 to 64
- values: bfloat16 [8192, 1024], P(('grp', 'seq')), parts along dimension 0, may hold values from -6 to 6
- doc_lengths: int32 [24], P('grp'), parts along dimension 0, may hold values from 1 to 8, 16 in all
Outputs:
- attended: bfloat16 [8192, 4096], P(('grp', 'seq')), parts along dimension 0
There are 4 independent parts, one for each index of `grp`. A program takes and returns all parts, laid end to end along the dimension named above; each array names one. Nothing has to cross between parts.
Inputs may be any that keep to these rules, and one draw needn't show every extreme that they name: `doc_lengths`: lengths of the documents in units of 128 tokens, summing to 16.
All inputs are finite; a program needn't handle non-finite values.
Results may differ from a plain program's by a relative error of at most 0.004.
Values may be sent and summed in bfloat16 or wider, within the bound.
No kernel may reach another device: no remote copies, remote signals or barrier semaphores. Data moves between devices by JAX's collectives and lax.ppermute only.
A program may use at most 128 MiB of HBM per device.

v0:
```python
import jax
import jax.numpy as jnp
from jax import lax
from jax.sharding import PartitionSpec as P

HEAD_DIM = 128
DOC_UNIT = 128
lowest = -1e30


def doc_starts(doc_lengths):
    lengths = doc_lengths * DOC_UNIT
    return jnp.cumsum(lengths) - lengths


def doc_ids(positions, starts):
    return jnp.sum((positions[:, None] >= starts[None, :]).astype(jnp.int32), axis=1)


def pick_width(total_rows, unit_rows):
    shard_count = total_rows // unit_rows
    most_factor = max(1, 1024 // unit_rows)
    chosen = 1
    for factor in range(1, most_factor + 1):
        if shard_count % factor == 0:
            chosen = factor
    return unit_rows * chosen


def fresh_state(kv_count, group_size, query_rows, head_dim):
    maxima = jnp.full((kv_count, group_size, query_rows), lowest, jnp.float32)
    totals = jnp.zeros((kv_count, group_size, query_rows), jnp.float32)
    accumulated = jnp.zeros((kv_count, group_size, query_rows, head_dim), jnp.float32)
    return (maxima, totals, accumulated)


def update(running, query_rows, query_pos, query_doc, key_part, value_part, key_pos, key_doc):
    scale = query_rows.shape[-1] ** (-0.5)
    needed = (
        (key_pos[0] <= query_pos[-1])
        & (key_doc[-1] >= query_doc[0])
        & (key_doc[0] <= query_doc[-1])
    )

    def compute(current):
        maxima, totals, accumulated = current
        allowed = (key_pos[None, :] <= query_pos[:, None]) & (
            key_doc[None, :] == query_doc[:, None]
        )
        scores = (
            jnp.einsum("qhgd,khd->hgqk", query_rows, key_part, preferred_element_type=jnp.float32)
            * scale
        )
        scores = jnp.where(allowed[None, None], scores, lowest)
        new_max = jnp.maximum(maxima, jnp.max(scores, axis=-1))
        weights = jnp.where(allowed[None, None], jnp.exp(scores - new_max[..., None]), 0.0)
        rescale = jnp.exp(maxima - new_max)
        totals = totals * rescale + jnp.sum(weights, axis=-1)
        mixed = jnp.einsum(
            "hgqk,khd->hgqd",
            weights.astype(jnp.bfloat16),
            value_part,
            preferred_element_type=jnp.float32,
        )
        accumulated = accumulated * rescale[..., None] + mixed
        return (new_max, totals, accumulated)

    def unchanged(current):
        return current

    return lax.cond(needed, compute, unchanged, running)


def sweep_keys(
    running, query_rows, query_pos, query_doc, key_rows, value_rows, key_start, all_docs, unit_rows
):
    total_rows = key_rows.shape[0]
    block_rows = pick_width(total_rows, unit_rows)
    turns = total_rows // block_rows

    def advance(number, current):
        offset = number * block_rows
        key_part = lax.dynamic_slice_in_dim(key_rows, offset, block_rows, 0)
        value_part = lax.dynamic_slice_in_dim(value_rows, offset, block_rows, 0)
        first_key = (key_start + offset).astype(jnp.int32)
        key_pos = first_key + jnp.arange(block_rows, dtype=jnp.int32)
        key_doc = lax.dynamic_slice_in_dim(all_docs, first_key, block_rows, 0)
        return update(
            current, query_rows, query_pos, query_doc, key_part, value_part, key_pos, key_doc
        )

    return lax.fori_loop(0, turns, advance, running)


def finish(running):
    maxima, totals, accumulated = running
    result = accumulated / totals[..., None]
    kv_count, group_size, query_rows, head_dim = result.shape
    return (
        result.transpose(2, 0, 1, 3)
        .reshape(query_rows, kv_count * group_size * head_dim)
        .astype(jnp.bfloat16)
    )


def on_device(queries, keys, values, doc_lengths):
    row_count = queries.shape[0]
    head_dim = HEAD_DIM
    kv_total = keys.shape[1] // head_dim
    heads_total = queries.shape[1] // head_dim
    group_size = heads_total // kv_total
    seq_count = lax.axis_size("seq")
    starts = doc_starts(doc_lengths)
    every_pos = jnp.arange(row_count * seq_count, dtype=jnp.int32)
    all_docs = doc_ids(every_pos, starts)
    heads_dev = heads_total // seq_count
    kv_dev = max(1, heads_dev // group_size)
    repeat_count = max(1, group_size // heads_dev)
    sub_group = heads_dev // kv_dev
    key_send = jnp.repeat(
        keys.reshape(row_count, kv_total, head_dim), repeat_count, axis=1
    ).reshape(row_count, seq_count * kv_dev * head_dim)
    value_send = jnp.repeat(
        values.reshape(row_count, kv_total, head_dim), repeat_count, axis=1
    ).reshape(row_count, seq_count * kv_dev * head_dim)
    all_queries, all_keys, all_values = (
        lax.all_to_all(queries, "seq", split_axis=1, concat_axis=0, tiled=True),
        lax.all_to_all(key_send, "seq", split_axis=1, concat_axis=0, tiled=True),
        lax.all_to_all(value_send, "seq", split_axis=1, concat_axis=0, tiled=True),
    )
    total_rows = all_queries.shape[0]
    all_keys = all_keys.reshape(total_rows, kv_dev, head_dim)
    all_values = all_values.reshape(total_rows, kv_dev, head_dim)
    block_rows = pick_width(total_rows, row_count)
    block_count = total_rows // block_rows
    query_blocks = all_queries.reshape(block_count, block_rows, kv_dev, sub_group, head_dim)

    def attend_block(inputs):
        query_part, number = inputs
        first_query = number * block_rows
        query_pos = first_query + jnp.arange(block_rows, dtype=jnp.int32)
        query_doc = lax.dynamic_slice_in_dim(all_docs, first_query, block_rows, 0)
        running = sweep_keys(
            fresh_state(kv_dev, sub_group, block_rows, head_dim),
            query_part,
            query_pos,
            query_doc,
            all_keys,
            all_values,
            0,
            all_docs,
            row_count,
        )
        return finish(running)

    outputs = lax.map(attend_block, (query_blocks, jnp.arange(block_count, dtype=jnp.int32)))
    outputs = outputs.reshape(total_rows, heads_dev * head_dim)
    return lax.all_to_all(outputs, "seq", split_axis=0, concat_axis=1, tiled=True)


def solution(mesh):
    placed = (P(("grp", "seq"), None), P(("grp", "seq"), None), P(("grp", "seq"), None), P("grp"))
    return jax.shard_map(
        on_device, mesh=mesh, in_specs=placed, out_specs=P(("grp", "seq"), None), check_vma=False
    )
```

profile of v0, /device:TPU:0, one launch (start us, length us, event | category | flops | bytes accessed | tf_op | source)
XLA Modules:
  0.0 189.1 jit_solution(11757262031421590637)
XLA Ops:
  0.0 1.0 copy-done
  1.0 0.9 copy_bitcast_fusion.3
  1.9 5.2 %all-to-all-start.1 = ((bf16[256,8,128]{2,0,1:T(8,128)(2,1)}), bf16[256,8,128]{2,0,1:T(8,128)(2,1)S(1)}, u32[]{:S(2)}, u32[]{:S(2)}) async-start(bf16[256,8,128]{2,0,1:T(8,128)(2,1)} %copy_bitcast_fusion.3), calls=%async_computation.1 | async-start | bytes 1048576 | tf_op jit(solution)/shard_map/all_to_all | solution.py:128
  7.1 3.1 %copy.49 = bf16[32,8,8,512]{3,2,0,1:T(8,128)(2,1)} copy(bf16[32,8,8,512]{3,2,1,0:T(8,128)(2,1)} %bitcast.104) | data formatting | bytes 4194304 | tf_op jit(solution)/shard_map/all_to_all | solution.py:127
  10.3 6.6 %all-to-all-done.1 = bf16[256,8,128]{2,0,1:T(8,128)(2,1)S(1)} async-done(((bf16[256,8,128]{2,0,1:T(8,128)(2,1)}), bf16[256,8,128]{2,0,1:T(8,128)(2,1)S(1)}, u32[]{:S(2)}, u32[]{:S(2)}) %all-to-all-start.1) | async-done | bytes 524320 | tf_op jit(solution)/shard_map/all_to_all | solution.py:128
  16.8 3.6 %all-to-all-start = ((bf16[256,8,512]{2,0,1:T(8,128)(2,1)}), bf16[256,8,512]{2,0,1:T(8,128)(2,1)S(1)}, u32[]{:S(2)}, u32[]{:S(2)}) async-start(bf16[256,8,512]{2,0,1:T(8,128)(2,1)} %bitcast.102), calls=%async_computation | async-start | bytes 4194304 | tf_op jit(solution)/shard_map/all_to_all | solution.py:127
  20.5 1.9 %copy_bitcast_fusion.2 = bf16[256,8,128]{2,0,1:T(8,128)(2,1)} fusion(bf16[256,1024]{1,0:T(8,128)(2,1)} %param.12), kind=kLoop, calls=%fused_computation.33 | loop fusion | bytes 1048576 | tf_op jit(solution)/shard_map/all_to_all | solution.py:129
  22.4 24.6 %all-to-all-done = bf16[256,8,512]{2,0,1:T(8,128)(2,1)S(1)} async-done(((bf16[256,8,512]{2,0,1:T(8,128)(2,1)}), bf16[256,8,512]{2,0,1:T(8,128)(2,1)S(1)}, u32[]{:S(2)}, u32[]{:S(2)}) %all-to-all-start) | async-done | bytes 2097184 | tf_op jit(solution)/shard_map/all_to_all | solution.py:127
  47.0 4.1 %all-to-all-start.2 = ((bf16[256,8,128]{2,0,1:T(8,128)(2,1)}), bf16[256,8,128]{2,0,1:T(8,128)(2,1)}, u32[]{:S(2)}, u32[]{:S(2)}) async-start(bf16[256,8,128]{2,0,1:T(8,128)(2,1)} %copy_bitcast_fusion.2), calls=%async_computation.2 | async-start | bytes 1048576 | tf_op jit(solution)/shard_map/all_to_all | solution.py:129
  51.5 2.1 %reshape.181 = bf16[2,1024,1,4,128]{4,3,1,0,2:T(4,128)(2,1)} reshape(bf16[8,256,512]{2,1,0:T(8,128)(2,1)S(1)} %bitcast.101) | data formatting | bytes 4194304 | tf_op jit(solution)/shard_map/reshape | solution.py:136
  53.6 7.3 %all-to-all-done.2 = bf16[256,8,128]{2,0,1:T(8,128)(2,1)} async-done(((bf16[256,8,128]{2,0,1:T(8,128)(2,1)}), bf16[256,8,128]{2,0,1:T(8,128)(2,1)}, u32[]{:S(2)}, u32[]{:S(2)}) %all-to-all-start.2) | async-done | bytes 524320 | tf_op jit(solution)/shard_map/all_to_all | solution.py:129
  61.5 91.1 %while.28 = (s32[]{:T(128)}, bf16[2,1024,512]{2,1,0:T(8,128)(2,1)}, s32[2]{0:T(128)}, s32[2048]{0:T(1024)S(1)}, bf16[2,1024,1,4,128]{4,3,1,0,2:T(4,128)(2,1)}, /...) while((s32[]{:T(128)}, bf16[2,1024,512]{2,1,0:T(8,128)(2,1)}, ...), condition=%wide.region_9.10_spmd, body=%wide.region_2.9_spmd.sunk | while | flops 2207266816 | bytes 93153088 | solution.py:156
  61.5 1.3 dynamic_slice.58
  63.5 1.6 constant_dynamic-slice_fusion.2
  65.2 1.4 broadcast.86
  66.7 27.9 %while.29 = (s32[]{:T(128)}, f32[1,4,1024]{2,1,0:T(4,128)S(1)}, f32[1,4,1024]{2,1,0:T(4,128)S(1)}, f32[1,4,1024,128]{3,2,1,0:T(8,128)}, s32[1024]{0:T(1024)S(1)}...) while((s32[]{:T(128)}, f32[1,4,1024]{2,1,0:T(4,128)S(1)}, ...), condition=%wide.region_8.8_spmd, body=%wide.region_3.7_spmd.sunk | while | flops 2206217216 | bytes 77362136 | solution.py:92
  72.5 16.3 %conditional.2 = ((f32[1,4,1024]{2,1,0:T(4,128)S(1)}, f32[1,4,1024]{2,1,0:T(4,128)S(1)}, f32[1,4,1024,128]{3,2,1,0:T(8,128)})) conditional(s32[]{:T(128)} %bitcast.95, (f32[1,4,1024]{2,1,0:T(4,128)S(1)}, f32[1,4,1024]{2,1,0:T(4,128)S(1)}, f32[1,4,1024,128]{3,2,1,0:T(8,128)}) %tuple.69, (s32[1024]{0:T(1024)S(1)}, s32[1024]{0:T(1024)S(1)}, ...), branch_computations={%region_4.3_spmd, %region_5.6_spmd} | conditional | flops 2206216192 | bytes 77349464 | solution.py:71
  72.5 1.2 compare_and_fusion
  73.7 3.1 %fusion = (f32[4,1024]{1,0:T(4,128)S(1)}, f32[1024,1024,4]{1,0,2:T(8,128)S(1)}) fusion(pred[1024,1024]{0,1:T(8,128)(4,1)S(1)} %compare_and_fusion, bf16[1024,1,4,128]{3,0,2,1:T(8,128)(2,1)S(1)} %get-tuple-element.284, bf16[2048,1,128]{2,0,1:T(8,128)(2,1)S(1)} %get-tuple-element.282, s32[]{:T(128)} %get-tuple-element.283), kind=kOutput, calls=%fused_computation.2 | convolution fusion | flops 1086320640 | bytes 19152900 | tf_op jit(solution)/shard_map/while/body/eval_jaxpr/while/body/eval_jaxpr/cond/branch_1_fun/qhgd,khd->hgqk/dot_general | solution.py:51
  76.9 4.2 %fusion.2 = f32[4,1024]{1,0:T(4,128)S(1)} fusion(f32[1024,1024,4]{1,0,2:T(8,128)S(1)} %get-tuple-element.379, f32[4,1024]{1,0:T(4,128)S(1)} %bitcast.97, pred[1024,1024]{0,1:T(8,128)(4,1)S(1)} %compare_and_fusion), kind=kLoop, calls=%fused_computation.4 | loop fusion | flops 20967424 | bytes 17858560 | tf_op jit(solution)/shard_map/while/body/eval_jaxpr/while/body/eval_jaxpr/cond/branch_1_fun/reduce_sum | solution.py:58
  81.1 6.4 %bitcast_add_fusion = f32[1,4,1024,128]{3,2,1,0:T(8,128)S(1)} fusion(f32[1,4,1024,128]{3,2,1,0:T(8,128)S(1)} %copy-done.1, f32[1024,1024,4]{1,0,2:T(8,128)S(1)} %get-tuple-element.379, f32[4,1024]{1,0:T(4,128)S(1)} %bitcast.98, pred[1024,1024]{0,1:T(8,128)(4,1)S(1)} %compare_and_fusion, f32[4,1024]{1,0:T(4,128)S(1)} %get-tuple-element.376, ...), kind=kOutput, calls=%fused_computation.9 | convolution fusion | flops 1095761920 | bytes 22315520 | tf_op jit(solution)/shard_map/while/body/eval_jaxpr/while/body/eval_jaxpr/cond/branch_1_fun/hgqk,khd->hgqd/dot_general | solution.py:59
  87.5 1.3 copy-done.2
  88.8 0.7 fusion.29
  94.6 2.0 %fusion.28 = bf16[1024,1,4,128]{3,0,2,1:T(8,128)(2,1)S(1)} fusion(f32[1,4,1024,128]{3,2,1,0:T(8,128)} %get-tuple-element.510, f32[4,1024]{1,0:T(4,128)S(1)} %bitcast.100), kind=kLoop, calls=%fused_computation.28.clone.1 | loop fusion | flops 1048576 | bytes 3162112 | tf_op jit(solution)/shard_map/while/body/eval_jaxpr/convert_element_type | solution.py:102
  96.6 0.8 copy.53
  97.8 1.0 constant_dynamic-update-slice_fusion.2
  98.9 1.3 dynamic_slice.58
  100.9 1.6 constant_dynamic-slice_fusion.2
  102.7 1.4 broadcast.86
  104.1 44.2 %while.29 = (s32[]{:T(128)}, f32[1,4,1024]{2,1,0:T(4,128)S(1)}, f32[1,4,1024]{2,1,0:T(4,128)S(1)}, f32[1,4,1024,128]{3,2,1,0:T(8,128)}, s32[1024]{0:T(1024)S(1)}...) while((s32[]{:T(128)}, f32[1,4,1024]{2,1,0:T(4,128)S(1)}, ...), condition=%wide.region_8.8_spmd, body=%wide.region_3.7_spmd.sunk | while | flops 2206217216 | bytes 77362136 | solution.py:92
  109.9 16.3 %conditional.2 = ((f32[1,4,1024]{2,1,0:T(4,128)S(1)}, f32[1,4,1024]{2,1,0:T(4,128)S(1)}, f32[1,4,1024,128]{3,2,1,0:T(8,128)})) conditional(s32[]{:T(128)} %bitcast.95, (f32[1,4,1024]{2,1,0:T(4,128)S(1)}, f32[1,4,1024]{2,1,0:T(4,128)S(1)}, f32[1,4,1024,128]{3,2,1,0:T(8,128)}) %tuple.69, (s32[1024]{0:T(1024)S(1)}, s32[1024]{0:T(1024)S(1)}, ...), branch_computations={%region_4.3_spmd, %region_5.6_spmd} | conditional | flops 2206216192 | bytes 77349464 | solution.py:71
  109.9 1.2 compare_and_fusion
  111.1 3.1 %fusion = (f32[4,1024]{1,0:T(4,128)S(1)}, f32[1024,1024,4]{1,0,2:T(8,128)S(1)}) fusion(pred[1024,1024]{0,1:T(8,128)(4,1)S(1)} %compare_and_fusion, bf16[1024,1,4,128]{3,0,2,1:T(8,128)(2,1)S(1)} %get-tuple-element.284, bf16[2048,1,128]{2,0,1:T(8,128)(2,1)S(1)} %get-tuple-element.282, s32[]{:T(128)} %get-tuple-element.283), kind=kOutput, calls=%fused_computation.2 | convolution fusion | flops 1086320640 | bytes 19152900 | tf_op jit(solution)/shard_map/while/body/eval_jaxpr/while/body/eval_jaxpr/cond/branch_1_fun/qhgd,khd->hgqk/dot_general | solution.py:51
  114.3 4.2 %fusion.2 = f32[4,1024]{1,0:T(4,128)S(1)} fusion(f32[1024,1024,4]{1,0,2:T(8,128)S(1)} %get-tuple-element.379, f32[4,1024]{1,0:T(4,128)S(1)} %bitcast.97, pred[1024,1024]{0,1:T(8,128)(4,1)S(1)} %compare_and_fusion), kind=kLoop, calls=%fused_computation.4 | loop fusion | flops 20967424 | bytes 17858560 | tf_op jit(solution)/shard_map/while/body/eval_jaxpr/while/body/eval_jaxpr/cond/branch_1_fun/reduce_sum | solution.py:58
  118.5 6.4 %bitcast_add_fusion = f32[1,4,1024,128]{3,2,1,0:T(8,128)S(1)} fusion(f32[1,4,1024,128]{3,2,1,0:T(8,128)S(1)} %copy-done.1, f32[1024,1024,4]{1,0,2:T(8,128)S(1)} %get-tuple-element.379, f32[4,1024]{1,0:T(4,128)S(1)} %bitcast.98, pred[1024,1024]{0,1:T(8,128)(4,1)S(1)} %compare_and_fusion, f32[4,1024]{1,0:T(4,128)S(1)} %get-tuple-element.376, ...), kind=kOutput, calls=%fused_computation.9 | convolution fusion | flops 1095761920 | bytes 22315520 | tf_op jit(solution)/shard_map/while/body/eval_jaxpr/while/body/eval_jaxpr/cond/branch_1_fun/hgqk,khd->hgqd/dot_general | solution.py:59
  124.9 1.3 copy-done.2
  132.0 16.3 %conditional.2 = ((f32[1,4,1024]{2,1,0:T(4,128)S(1)}, f32[1,4,1024]{2,1,0:T(4,128)S(1)}, f32[1,4,1024,128]{3,2,1,0:T(8,128)})) conditional(s32[]{:T(128)} %bitcast.95, (f32[1,4,1024]{2,1,0:T(4,128)S(1)}, f32[1,4,1024]{2,1,0:T(4,128)S(1)}, f32[1,4,1024,128]{3,2,1,0:T(8,128)}) %tuple.69, (s32[1024]{0:T(1024)S(1)}, s32[1024]{0:T(1024)S(1)}, ...), branch_computations={%region_4.3_spmd, %region_5.6_spmd} | conditional | flops 2206216192 | bytes 77349464 | solution.py:71
  132.0 1.2 compare_and_fusion
  133.2 3.1 %fusion = (f32[4,1024]{1,0:T(4,128)S(1)}, f32[1024,1024,4]{1,0,2:T(8,128)S(1)}) fusion(pred[1024,1024]{0,1:T(8,128)(4,1)S(1)} %compare_and_fusion, bf16[1024,1,4,128]{3,0,2,1:T(8,128)(2,1)S(1)} %get-tuple-element.284, bf16[2048,1,128]{2,0,1:T(8,128)(2,1)S(1)} %get-tuple-element.282, s32[]{:T(128)} %get-tuple-element.283), kind=kOutput, calls=%fused_computation.2 | convolution fusion | flops 1086320640 | bytes 19152900 | tf_op jit(solution)/shard_map/while/body/eval_jaxpr/while/body/eval_jaxpr/cond/branch_1_fun/qhgd,khd->hgqk/dot_general | solution.py:51
  136.4 4.2 %fusion.2 = f32[4,1024]{1,0:T(4,128)S(1)} fusion(f32[1024,1024,4]{1,0,2:T(8,128)S(1)} %get-tuple-element.379, f32[4,1024]{1,0:T(4,128)S(1)} %bitcast.97, pred[1024,1024]{0,1:T(8,128)(4,1)S(1)} %compare_and_fusion), kind=kLoop, calls=%fused_computation.4 | loop fusion | flops 20967424 | bytes 17858560 | tf_op jit(solution)/shard_map/while/body/eval_jaxpr/while/body/eval_jaxpr/cond/branch_1_fun/reduce_sum | solution.py:58
  140.6 6.4 %bitcast_add_fusion = f32[1,4,1024,128]{3,2,1,0:T(8,128)S(1)} fusion(f32[1,4,1024,128]{3,2,1,0:T(8,128)S(1)} %copy-done.1, f32[1024,1024,4]{1,0,2:T(8,128)S(1)} %get-tuple-element.379, f32[4,1024]{1,0:T(4,128)S(1)} %bitcast.98, pred[1024,1024]{0,1:T(8,128)(4,1)S(1)} %compare_and_fusion, f32[4,1024]{1,0:T(4,128)S(1)} %get-tuple-element.376, ...), kind=kOutput, calls=%fused_computation.9 | convolution fusion | flops 1095761920 | bytes 22315520 | tf_op jit(solution)/shard_map/while/body/eval_jaxpr/while/body/eval_jaxpr/cond/branch_1_fun/hgqk,khd->hgqd/dot_general | solution.py:59
  147.0 1.3 copy-done.2
  148.3 2.0 %fusion.28 = bf16[1024,1,4,128]{3,0,2,1:T(8,128)(2,1)S(1)} fusion(f32[1,4,1024,128]{3,2,1,0:T(8,128)} %get-tuple-element.510, f32[4,1024]{1,0:T(4,128)S(1)} %bitcast.100), kind=kLoop, calls=%fused_computation.28.clone.1 | loop fusion | flops 1048576 | bytes 3162112 | tf_op jit(solution)/shard_map/while/body/eval_jaxpr/convert_element_type | solution.py:102
  150.3 0.8 copy.53
  151.6 1.0 constant_dynamic-update-slice_fusion.2
  152.6 30.1 %all_to_all.67 = bf16[8,256,512]{2,1,0:T(8,128)(2,1)S(1)} all-to-all(bf16[8,256,512]{2,1,0:T(8,128)(2,1)} %bitcast.105), channel_id=1, replica_groups=mesh['seq'=8,'grp'=4] {'seq'}, dimensions={0} | all-to-all | bytes 4194304 | tf_op jit(solution)/shard_map/all_to_all | solution.py:158
  182.7 2.4 %copy.37 = bf16[8,256,512]{1,2,0:T(8,128)(2,1)} copy(bf16[8,256,512]{2,1,0:T(8,128)(2,1)S(1)} %all_to_all.67) | data formatting | bytes 4194304 | tf_op jit(solution)/shard_map/all_to_all | solution.py:158
  185.1 4.1 %copy.38 = bf16[256,4096]{1,0:T(8,128)(2,1)} copy(bf16[256,4096]{0,1:T(8,128)(2,1)} %bitcast.103) | data formatting | bytes 4194304 | tf_op jit(solution)/shard_map/all_to_all | solution.py:158
  (59 shorter events, 9.0 us)
Async XLA Ops:
  0.0 1.0 copy-start
  1.9 14.9 %all-to-all-start.1 = ((bf16[256,8,128]{2,0,1:T(8,128)(2,1)}), bf16[256,8,128]{2,0,1:T(8,128)(2,1)S(1)}, u32[]{:S(2)}, u32[]{:S(2)}) async-start(bf16[256,8,128]{2,0,1:T(8,128)(2,1)} %copy_bitcast_fusion.3), calls=%async_computation.1 | async-start | bytes 1048576 | tf_op jit(solution)/shard_map/all_to_all | solution.py:128
  10.3 40.9 %copy-start.3 = (s32[6]{0:T(128)S(1)}, s32[6]{0:T(128)}, u32[]{:S(2)}) copy-start(s32[6]{0:T(128)} %param.13) | copy-start | bytes 76
  16.8 30.2 %all-to-all-start = ((bf16[256,8,512]{2,0,1:T(8,128)(2,1)}), bf16[256,8,512]{2,0,1:T(8,128)(2,1)S(1)}, u32[]{:S(2)}, u32[]{:S(2)}) async-start(bf16[256,8,512]{2,0,1:T(8,128)(2,1)} %bitcast.102), calls=%async_computation | async-start | bytes 4194304 | tf_op jit(solution)/shard_map/all_to_all | solution.py:127
  47.0 13.9 %all-to-all-start.2 = ((bf16[256,8,128]{2,0,1:T(8,128)(2,1)}), bf16[256,8,128]{2,0,1:T(8,128)(2,1)}, u32[]{:S(2)}, u32[]{:S(2)}) async-start(bf16[256,8,128]{2,0,1:T(8,128)(2,1)} %copy_bitcast_fusion.2), calls=%async_computation.2 | async-start | bytes 1048576 | tf_op jit(solution)/shard_map/all_to_all | solution.py:129
  76.9 4.2 %copy-start.1 = (f32[1,4,1024,128]{3,2,1,0:T(8,128)S(1)}, f32[1,4,1024,128]{3,2,1,0:T(8,128)}, u32[]{:S(2)}) copy-start(f32[1,4,1024,128]{3,2,1,0:T(8,128)} %get-tuple-element.286) | copy-start | bytes 6291460 | tf_op jit(solution)/shard_map/while/body/eval_jaxpr/while/body/eval_jaxpr/cond
  87.5 1.3 copy-start.2
  114.3 4.2 %copy-start.1 = (f32[1,4,1024,128]{3,2,1,0:T(8,128)S(1)}, f32[1,4,1024,128]{3,2,1,0:T(8,128)}, u32[]{:S(2)}) copy-start(f32[1,4,1024,128]{3,2,1,0:T(8,128)} %get-tuple-element.286) | copy-start | bytes 6291460 | tf_op jit(solution)/shard_map/while/body/eval_jaxpr/while/body/eval_jaxpr/cond
  124.9 1.3 copy-start.2
  136.4 4.2 %copy-start.1 = (f32[1,4,1024,128]{3,2,1,0:T(8,128)S(1)}, f32[1,4,1024,128]{3,2,1,0:T(8,128)}, u32[]{:S(2)}) copy-start(f32[1,4,1024,128]{3,2,1,0:T(8,128)} %get-tuple-element.286) | copy-start | bytes 6291460 | tf_op jit(solution)/shard_map/while/body/eval_jaxpr/while/body/eval_jaxpr/cond
  147.0 1.3 copy-start.2
where the time goes:
time: 190 us; the launch traced here: 189 us
  local copies, waits for them, and re-layouts  41.2 us (22%)
  waiting for transfers between devices  38.5 us (20%)
  blocking collectives  30.1 us (16%)
  matrix products  28.5 us (15%)
  other arithmetic  20.5 us (11%)
  loops' own time  17.4 us (9%)
  starting transfers between devices  13 us (7%)
    all_to_all x1, blocking collectives, on_device(): lax.all_to_all(outputs, 'seq', split_axis=0, concat_axis=1, tiled=True)  30.1 us
    all_to_all x1, waiting for transfers between devices, on_device(): lax.all_to_all(queries, 'seq', split_axis=1, concat_axis=0, tiled=True)  24.6 us
    dot_general x3, matrix products, compute(): jnp.einsum('hgqk,khd->hgqd', weights.astype(jnp.bfloat16), value_part, pr...  19.1 us
    another operation x2, loops' own time, sweep_keys(): return lax.fori_loop(0, turns, advance, running)  15.7 us
    reduce_sum x3, other arithmetic, compute(): totals = totals * rescale + jnp.sum(weights, axis=-1)  12.6 us
    dot_general x3, matrix products, compute(): jnp.einsum('qhgd,khd->hgqk', query_rows, key_part, preferred_element_type...  9.44 us
    all_to_all x1, waiting for transfers between devices, on_device(): lax.all_to_all(value_send, 'seq', split_axis=1, concat_axis=0, tiled=True)  7.32 us
    all_to_all x1, waiting for transfers between devices, on_device(): lax.all_to_all(key_send, 'seq', split_axis=1, concat_axis=0, tiled=True)  6.57 us
  transfers between devices with their start and end apart: 3, of which 3 were waited for; matrix products, arithmetic and copies ran while one was open for 4% of the time, Pallas kernels for 0%

commit v1 on v0

--- a/solution.py
+++ b/solution.py
@@ -125,7 +125,12 @@
     ).reshape(row_count, seq_count * kv_dev * head_dim)
     all_queries, all_keys, all_values = (
         lax.all_to_all(queries, "seq", split_axis=1, concat_axis=0, tiled=True),
-        lax.all_to_all(key_send, "seq", split_axis=1, concat_axis=0, tiled=True),
+        jnp.concatenate(
+            lax.all_to_all(
+                jnp.stack(jnp.split(key_send, lax.axis_size("seq"), axis=1)), "seq", 0, 0
+            ),
+            axis=0,
+        ),
         lax.all_to_all(value_send, "seq", split_axis=1, concat_axis=0, tiled=True),
     )
     total_rows = all_queries.shape[0]

time: 190 us -> 200 us (1.053)
  local copies, waits for them, and re-layouts: 41.2 us -> 50 us
    unnamed x4 -> x11, local copies, waits for them, and re-layouts: 1.05 us -> 10.4 us
    another operation x6 -> x7, local copies, waits for them, and re-layouts: 2.91 us -> 4.38 us
  transfers between devices with their start and end apart: 3 -> 3, of which waited for: 3 -> 3; matrix products, arithmetic and copies ran while one was open for 4% -> 3% of each run, Pallas kernels for 0% -> 0%
where the time goes in v1:
time: 200 us; the launch traced here: 199 us
  local copies, waits for them, and re-layouts  50 us (25%)
  waiting for transfers between devices  39.5 us (20%)
  blocking collectives  30.1 us (15%)
  matrix products  28.5 us (14%)
  other arithmetic  20.5 us (10%)
  loops' own time  17.4 us (9%)
  starting transfers between devices  13 us (6%)
    all_to_all x1, blocking collectives, on_device(): lax.all_to_all(outputs, 'seq', split_axis=0, concat_axis=1, tiled=True)  30.1 us
    all_to_all x1, waiting for transfers between devices, on_device(): lax.all_to_all(queries, 'seq', split_axis=1, concat_axis=0, tiled=True)  25.6 us
    dot_general x3, matrix products, compute(): jnp.einsum('hgqk,khd->hgqd', weights.astype(jnp.bfloat16), value_part, pr...  19.1 us
    another operation x2, loops' own time, sweep_keys(): return lax.fori_loop(0, turns, advance, running)  15.7 us
    reduce_sum x3, other arithmetic, compute(): totals = totals * rescale + jnp.sum(weights, axis=-1)  12.6 us
    unnamed x11, local copies, waits for them, and re-layouts  10.4 us
    dot_general x3, matrix products, compute(): jnp.einsum('qhgd,khd->hgqk', query_rows, key_part, preferred_element_type...  9.44 us
    all_to_all x1, waiting for transfers between devices, on_device(): lax.all_to_all(value_send, 'seq', split_axis=1, concat_axis=0, tiled=True)  7.32 us
  transfers between devices with their start and end apart: 3, of which 3 were waited for; matrix products, arithmetic and copies ran while one was open for 3% of the time, Pallas kernels for 0%

profile of v1, /device:TPU:0, one launch (start us, length us, event | category | flops | bytes accessed | tf_op | source)
XLA Modules:
  0.0 199.0 jit_solution(15180586394917760287)
XLA Ops:
  0.0 1.5 bitcast_dynamic-update-slice_fusion.7
  1.5 1.5 bitcast_dynamic-update-slice_fusion.6
  3.0 1.5 bitcast_dynamic-update-slice_fusion.5
  4.5 1.5 bitcast_dynamic-update-slice_fusion.4
  6.0 1.5 bitcast_dynamic-update-slice_fusion.3
  7.4 1.5 bitcast_dynamic-update-slice_fusion.2
  8.9 1.5 bitcast_dynamic-update-slice_fusion.1
  10.4 1.5 bitcast_dynamic-update-slice_fusion
  11.8 5.2 %all-to-all-start.1 = ((bf16[8,256,128]{2,1,0:T(8,128)(2,1)}), bf16[8,256,128]{2,1,0:T(8,128)(2,1)S(1)}, u32[]{:S(2)}, u32[]{:S(2)}) async-start(bf16[8,256,128]{2,1,0:T(8,128)(2,1)} %bitcast_dynamic-update-slice_fusion), calls=%async_computation.1 | async-start | bytes 1048576 | tf_op jit(solution)/shard_map/all_to_all | solution.py:129
  17.0 3.1 %copy.42 = bf16[32,8,8,512]{3,2,0,1:T(8,128)(2,1)} copy(bf16[32,8,8,512]{3,2,1,0:T(8,128)(2,1)} %bitcast.113) | data formatting | bytes 4194304 | tf_op jit(solution)/shard_map/all_to_all | solution.py:127
  20.2 6.6 %all-to-all-done.1 = bf16[8,256,128]{2,1,0:T(8,128)(2,1)S(1)} async-done(((bf16[8,256,128]{2,1,0:T(8,128)(2,1)}), bf16[8,256,128]{2,1,0:T(8,128)(2,1)S(1)}, u32[]{:S(2)}, u32[]{:S(2)}) %all-to-all-start.1) | async-done | bytes 524320 | tf_op jit(solution)/shard_map/all_to_all | solution.py:129
  26.8 3.6 %all-to-all-start = ((bf16[256,8,512]{2,0,1:T(8,128)(2,1)}), bf16[256,8,512]{2,0,1:T(8,128)(2,1)S(1)}, u32[]{:S(2)}, u32[]{:S(2)}) async-start(bf16[256,8,512]{2,0,1:T(8,128)(2,1)} %bitcast.111), calls=%async_computation | async-start | bytes 4194304 | tf_op jit(solution)/shard_map/all_to_all | solution.py:127
  31.3 25.6 %all-to-all-done = bf16[256,8,512]{2,0,1:T(8,128)(2,1)S(1)} async-done(((bf16[256,8,512]{2,0,1:T(8,128)(2,1)}), bf16[256,8,512]{2,0,1:T(8,128)(2,1)S(1)}, u32[]{:S(2)}, u32[]{:S(2)}) %all-to-all-start) | async-done | bytes 2097184 | tf_op jit(solution)/shard_map/all_to_all | solution.py:127
  56.9 4.1 %all-to-all-start.2 = ((bf16[256,8,128]{2,0,1:T(8,128)(2,1)}), bf16[256,8,128]{2,0,1:T(8,128)(2,1)}, u32[]{:S(2)}, u32[]{:S(2)}) async-start(bf16[256,8,128]{2,0,1:T(8,128)(2,1)} %copy_bitcast_fusion.2), calls=%async_computation.2 | async-start | bytes 1048576 | tf_op jit(solution)/shard_map/all_to_all | solution.py:134
  61.4 2.1 %reshape.174 = bf16[2,1024,1,4,128]{4,3,1,0,2:T(4,128)(2,1)} reshape(bf16[8,256,512]{2,1,0:T(8,128)(2,1)S(1)} %bitcast.110) | data formatting | bytes 4194304 | tf_op jit(solution)/shard_map/reshape | solution.py:141
  63.5 7.3 %all-to-all-done.2 = bf16[256,8,128]{2,0,1:T(8,128)(2,1)} async-done(((bf16[256,8,128]{2,0,1:T(8,128)(2,1)}), bf16[256,8,128]{2,0,1:T(8,128)(2,1)}, u32[]{:S(2)}, u32[]{:S(2)}) %all-to-all-start.2) | async-done | bytes 524320 | tf_op jit(solution)/shard_map/all_to_all | solution.py:134
  71.4 91.1 %while.28 = (s32[]{:T(128)}, bf16[2,1024,512]{2,1,0:T(8,128)(2,1)}, s32[2]{0:T(128)}, s32[2048]{0:T(1024)S(1)}, bf16[2,1024,1,4,128]{4,3,1,0,2:T(4,128)(2,1)}, /...) while((s32[]{:T(128)}, bf16[2,1024,512]{2,1,0:T(8,128)(2,1)}, ...), condition=%wide.region_9.10_spmd, body=%wide.region_2.9_spmd.sunk | while | flops 2207266816 | bytes 93153088 | solution.py:161
  71.4 1.3 dynamic_slice.58
  73.4 1.6 constant_dynamic-slice_fusion.2
  75.2 1.4 broadcast.86
  76.6 27.9 %while.29 = (s32[]{:T(128)}, f32[1,4,1024]{2,1,0:T(4,128)S(1)}, f32[1,4,1024]{2,1,0:T(4,128)S(1)}, f32[1,4,1024,128]{3,2,1,0:T(8,128)}, s32[1024]{0:T(1024)S(1)}...) while((s32[]{:T(128)}, f32[1,4,1024]{2,1,0:T(4,128)S(1)}, ...), condition=%wide.region_8.8_spmd, body=%wide.region_3.7_spmd.sunk | while | flops 2206217216 | bytes 77362136 | solution.py:92
  82.4 16.3 %conditional.2 = ((f32[1,4,1024]{2,1,0:T(4,128)S(1)}, f32[1,4,1024]{2,1,0:T(4,128)S(1)}, f32[1,4,1024,128]{3,2,1,0:T(8,128)})) conditional(s32[]{:T(128)} %bitcast.104, (f32[1,4,1024]{2,1,0:T(4,128)S(1)}, f32[1,4,1024]{2,1,0:T(4,128)S(1)}, f32[1,4,1024,128]{3,2,1,0:T(8,128)}) %tuple.69, (s32[1024]{0:T(1024)S(1)}, s32[1024]{0:T(1024)S(1)}, ...), branch_computations={%region_4.3_spmd, %region_5.6_spmd} | conditional | flops 2206216192 | bytes 77349464 | solution.py:71
  82.4 1.2 compare_and_fusion
  83.6 3.1 %fusion = (f32[4,1024]{1,0:T(4,128)S(1)}, f32[1024,1024,4]{1,0,2:T(8,128)S(1)}) fusion(pred[1024,1024]{0,1:T(8,128)(4,1)S(1)} %compare_and_fusion, bf16[1024,1,4,128]{3,0,2,1:T(8,128)(2,1)S(1)} %get-tuple-element.284, bf16[2048,1,128]{2,0,1:T(8,128)(2,1)S(1)} %get-tuple-element.282, s32[]{:T(128)} %get-tuple-element.283), kind=kOutput, calls=%fused_computation.2 | convolution fusion | flops 1086320640 | bytes 19152900 | tf_op jit(solution)/shard_map/while/body/eval_jaxpr/while/body/eval_jaxpr/cond/branch_1_fun/qhgd,khd->hgqk/dot_general | solution.py:51
  86.8 4.2 %fusion.2 = f32[4,1024]{1,0:T(4,128)S(1)} fusion(f32[1024,1024,4]{1,0,2:T(8,128)S(1)} %get-tuple-element.379, f32[4,1024]{1,0:T(4,128)S(1)} %bitcast.106, pred[1024,1024]{0,1:T(8,128)(4,1)S(1)} %compare_and_fusion), kind=kLoop, calls=%fused_computation.4 | loop fusion | flops 20967424 | bytes 17858560 | tf_op jit(solution)/shard_map/while/body/eval_jaxpr/while/body/eval_jaxpr/cond/branch_1_fun/reduce_sum | solution.py:58
  91.0 6.4 %bitcast_add_fusion = f32[1,4,1024,128]{3,2,1,0:T(8,128)S(1)} fusion(f32[1,4,1024,128]{3,2,1,0:T(8,128)S(1)} %copy-done.1, f32[1024,1024,4]{1,0,2:T(8,128)S(1)} %get-tuple-element.379, f32[4,1024]{1,0:T(4,128)S(1)} %bitcast.107, pred[1024,1024]{0,1:T(8,128)(4,1)S(1)} %compare_and_fusion, f32[4,1024]{1,0:T(4,128)S(1)} %get-tuple-element.376, ...), kind=kOutput, calls=%fused_computation.9 | convolution fusion | flops 1095761920 | bytes 22315520 | tf_op jit(solution)/shard_map/while/body/eval_jaxpr/while/body/eval_jaxpr/cond/branch_1_fun/hgqk,khd->hgqd/dot_general | solution.py:59
  97.4 1.3 copy-done.2
  104.5 2.0 fusion.27
  108.8 1.3 dynamic_slice.58
  110.8 1.6 constant_dynamic-slice_fusion.2
  112.6 1.4 broadcast.86
  114.0 44.2 %while.29 = (s32[]{:T(128)}, f32[1,4,1024]{2,1,0:T(4,128)S(1)}, f32[1,4,1024]{2,1,0:T(4,128)S(1)}, f32[1,4,1024,128]{3,2,1,0:T(8,128)}, s32[1024]{0:T(1024)S(1)}...) while((s32[]{:T(128)}, f32[1,4,1024]{2,1,0:T(4,128)S(1)}, ...), condition=%wide.region_8.8_spmd, body=%wide.region_3.7_spmd.sunk | while | flops 2206217216 | bytes 77362136 | solution.py:92
  119.8 16.3 %conditional.2 = ((f32[1,4,1024]{2,1,0:T(4,128)S(1)}, f32[1,4,1024]{2,1,0:T(4,128)S(1)}, f32[1,4,1024,128]{3,2,1,0:T(8,128)})) conditional(s32[]{:T(128)} %bitcast.104, (f32[1,4,1024]{2,1,0:T(4,128)S(1)}, f32[1,4,1024]{2,1,0:T(4,128)S(1)}, f32[1,4,1024,128]{3,2,1,0:T(8,128)}) %tuple.69, (s32[1024]{0:T(1024)S(1)}, s32[1024]{0:T(1024)S(1)}, ...), branch_computations={%region_4.3_spmd, %region_5.6_spmd} | conditional | flops 2206216192 | bytes 77349464 | solution.py:71
  119.8 1.2 compare_and_fusion
  121.0 3.1 %fusion = (f32[4,1024]{1,0:T(4,128)S(1)}, f32[1024,1024,4]{1,0,2:T(8,128)S(1)}) fusion(pred[1024,1024]{0,1:T(8,128)(4,1)S(1)} %compare_and_fusion, bf16[1024,1,4,128]{3,0,2,1:T(8,128)(2,1)S(1)} %get-tuple-element.284, bf16[2048,1,128]{2,0,1:T(8,128)(2,1)S(1)} %get-tuple-element.282, s32[]{:T(128)} %get-tuple-element.283), kind=kOutput, calls=%fused_computation.2 | convolution fusion | flops 1086320640 | bytes 19152900 | tf_op jit(solution)/shard_map/while/body/eval_jaxpr/while/body/eval_jaxpr/cond/branch_1_fun/qhgd,khd->hgqk/dot_general | solution.py:51
  124.2 4.2 %fusion.2 = f32[4,1024]{1,0:T(4,128)S(1)} fusion(f32[1024,1024,4]{1,0,2:T(8,128)S(1)} %get-tuple-element.379, f32[4,1024]{1,0:T(4,128)S(1)} %bitcast.106, pred[1024,1024]{0,1:T(8,128)(4,1)S(1)} %compare_and_fusion), kind=kLoop, calls=%fused_computation.4 | loop fusion | flops 20967424 | bytes 17858560 | tf_op jit(solution)/shard_map/while/body/eval_jaxpr/while/body/eval_jaxpr/cond/branch_1_fun/reduce_sum | solution.py:58
  128.5 6.4 %bitcast_add_fusion = f32[1,4,1024,128]{3,2,1,0:T(8,128)S(1)} fusion(f32[1,4,1024,128]{3,2,1,0:T(8,128)S(1)} %copy-done.1, f32[1024,1024,4]{1,0,2:T(8,128)S(1)} %get-tuple-element.379, f32[4,1024]{1,0:T(4,128)S(1)} %bitcast.107, pred[1024,1024]{0,1:T(8,128)(4,1)S(1)} %compare_and_fusion, f32[4,1024]{1,0:T(4,128)S(1)} %get-tuple-element.376, ...), kind=kOutput, calls=%fused_computation.9 | convolution fusion | flops 1095761920 | bytes 22315520 | tf_op jit(solution)/shard_map/while/body/eval_jaxpr/while/body/eval_jaxpr/cond/branch_1_fun/hgqk,khd->hgqd/dot_general | solution.py:59
  134.8 1.3 copy-done.2
  141.9 16.3 %conditional.2 = ((f32[1,4,1024]{2,1,0:T(4,128)S(1)}, f32[1,4,1024]{2,1,0:T(4,128)S(1)}, f32[1,4,1024,128]{3,2,1,0:T(8,128)})) conditional(s32[]{:T(128)} %bitcast.104, (f32[1,4,1024]{2,1,0:T(4,128)S(1)}, f32[1,4,1024]{2,1,0:T(4,128)S(1)}, f32[1,4,1024,128]{3,2,1,0:T(8,128)}) %tuple.69, (s32[1024]{0:T(1024)S(1)}, s32[1024]{0:T(1024)S(1)}, ...), branch_computations={%region_4.3_spmd, %region_5.6_spmd} | conditional | flops 2206216192 | bytes 77349464 | solution.py:71
  141.9 1.2 compare_and_fusion
  143.1 3.1 %fusion = (f32[4,1024]{1,0:T(4,128)S(1)}, f32[1024,1024,4]{1,0,2:T(8,128)S(1)}) fusion(pred[1024,1024]{0,1:T(8,128)(4,1)S(1)} %compare_and_fusion, bf16[1024,1,4,128]{3,0,2,1:T(8,128)(2,1)S(1)} %get-tuple-element.284, bf16[2048,1,128]{2,0,1:T(8,128)(2,1)S(1)} %get-tuple-element.282, s32[]{:T(128)} %get-tuple-element.283), kind=kOutput, calls=%fused_computation.2 | convolution fusion | flops 1086320640 | bytes 19152900 | tf_op jit(solution)/shard_map/while/body/eval_jaxpr/while/body/eval_jaxpr/cond/branch_1_fun/qhgd,khd->hgqk/dot_general | solution.py:51
  146.3 4.2 %fusion.2 = f32[4,1024]{1,0:T(4,128)S(1)} fusion(f32[1024,1024,4]{1,0,2:T(8,128)S(1)} %get-tuple-element.379, f32[4,1024]{1,0:T(4,128)S(1)} %bitcast.106, pred[1024,1024]{0,1:T(8,128)(4,1)S(1)} %compare_and_fusion), kind=kLoop, calls=%fused_computation.4 | loop fusion | flops 20967424 | bytes 17858560 | tf_op jit(solution)/shard_map/while/body/eval_jaxpr/while/body/eval_jaxpr/cond/branch_1_fun/reduce_sum | solution.py:58
  150.5 6.4 %bitcast_add_fusion = f32[1,4,1024,128]{3,2,1,0:T(8,128)S(1)} fusion(f32[1,4,1024,128]{3,2,1,0:T(8,128)S(1)} %copy-done.1, f32[1024,1024,4]{1,0,2:T(8,128)S(1)} %get-tuple-element.379, f32[4,1024]{1,0:T(4,128)S(1)} %bitcast.107, pred[1024,1024]{0,1:T(8,128)(4,1)S(1)} %compare_and_fusion, f32[4,1024]{1,0:T(4,128)S(1)} %get-tuple-element.376, ...), kind=kOutput, calls=%fused_computation.9 | convolution fusion | flops 1095761920 | bytes 22315520 | tf_op jit(solution)/shard_map/while/body/eval_jaxpr/while/body/eval_jaxpr/cond/branch_1_fun/hgqk,khd->hgqd/dot_general | solution.py:59
  156.9 1.3 copy-done.2
  158.2 2.0 fusion.27
  162.5 30.1 %all_to_all.56 = bf16[8,256,512]{2,1,0:T(8,128)(2,1)S(1)} all-to-all(bf16[8,256,512]{2,1,0:T(8,128)(2,1)} %bitcast.114), channel_id=1, replica_groups=mesh['seq'=8,'grp'=4] {'seq'}, dimensions={0} | all-to-all | bytes 4194304 | tf_op jit(solution)/shard_map/all_to_all | solution.py:163
  192.6 2.4 %copy.32 = bf16[8,256,512]{1,2,0:T(8,128)(2,1)} copy(bf16[8,256,512]{2,1,0:T(8,128)(2,1)S(1)} %all_to_all.56) | data formatting | bytes 4194304 | tf_op jit(solution)/shard_map/all_to_all | solution.py:163
  195.0 4.1 %copy.33 = bf16[256,4096]{1,0:T(8,128)(2,1)} copy(bf16[256,4096]{0,1:T(8,128)(2,1)} %bitcast.112) | data formatting | bytes 4194304 | tf_op jit(solution)/shard_map/all_to_all | solution.py:163
  (66 shorter events, 14.3 us)
Async XLA Ops:
  0.0 30.4 %copy-start = (bf16[256,1024]{1,0:T(8,128)(2,1)S(1)}, bf16[256,1024]{1,0:T(8,128)(2,1)}, u32[]{:S(2)}) copy-start(bf16[256,1024]{1,0:T(8,128)(2,1)} %param.12) | copy-start | bytes 1572868
  11.8 14.9 %all-to-all-start.1 = ((bf16[8,256,128]{2,1,0:T(8,128)(2,1)}), bf16[8,256,128]{2,1,0:T(8,128)(2,1)S(1)}, u32[]{:S(2)}, u32[]{:S(2)}) async-start(bf16[8,256,128]{2,1,0:T(8,128)(2,1)} %bitcast_dynamic-update-slice_fusion), calls=%async_computation.1 | async-start | bytes 1048576 | tf_op jit(solution)/shard_map/all_to_all | solution.py:129
  20.2 40.9 %copy-start.3 = (s32[6]{0:T(128)S(1)}, s32[6]{0:T(128)}, u32[]{:S(2)}) copy-start(s32[6]{0:T(128)} %param.13) | copy-start | bytes 76
  26.8 30.2 %all-to-all-start = ((bf16[256,8,512]{2,0,1:T(8,128)(2,1)}), bf16[256,8,512]{2,0,1:T(8,128)(2,1)S(1)}, u32[]{:S(2)}, u32[]{:S(2)}) async-start(bf16[256,8,512]{2,0,1:T(8,128)(2,1)} %bitcast.111), calls=%async_computation | async-start | bytes 4194304 | tf_op jit(solution)/shard_map/all_to_all | solution.py:127
  56.9 13.9 %all-to-all-start.2 = ((bf16[256,8,128]{2,0,1:T(8,128)(2,1)}), bf16[256,8,128]{2,0,1:T(8,128)(2,1)}, u32[]{:S(2)}, u32[]{:S(2)}) async-start(bf16[256,8,128]{2,0,1:T(8,128)(2,1)} %copy_bitcast_fusion.2), calls=%async_computation.2 | async-start | bytes 1048576 | tf_op jit(solution)/shard_map/all_to_all | solution.py:134
  86.8 4.2 %copy-start.1 = (f32[1,4,1024,128]{3,2,1,0:T(8,128)S(1)}, f32[1,4,1024,128]{3,2,1,0:T(8,128)}, u32[]{:S(2)}) copy-start(f32[1,4,1024,128]{3,2,1,0:T(8,128)} %get-tuple-element.286) | copy-start | bytes 6291460 | tf_op jit(solution)/shard_map/while/body/eval_jaxpr/while/body/eval_jaxpr/cond
  97.4 1.3 copy-start.2
  124.2 4.2 %copy-start.1 = (f32[1,4,1024,128]{3,2,1,0:T(8,128)S(1)}, f32[1,4,1024,128]{3,2,1,0:T(8,128)}, u32[]{:S(2)}) copy-start(f32[1,4,1024,128]{3,2,1,0:T(8,128)} %get-tuple-element.286) | copy-start | bytes 6291460 | tf_op jit(solution)/shard_map/while/body/eval_jaxpr/while/body/eval_jaxpr/cond
  134.8 1.3 copy-start.2
  146.3 4.2 %copy-start.1 = (f32[1,4,1024,128]{3,2,1,0:T(8,128)S(1)}, f32[1,4,1024,128]{3,2,1,0:T(8,128)}, u32[]{:S(2)}) copy-start(f32[1,4,1024,128]{3,2,1,0:T(8,128)} %get-tuple-element.286) | copy-start | bytes 6291460 | tf_op jit(solution)/shard_map/while/body/eval_jaxpr/while/body/eval_jaxpr/cond
  156.9 1.3 copy-start.2
